TPU v7x, 128 devices: a whole 4x4x4 slice. The times are simulated.
128 devices in a mesh: row: 8 (over z, core), col: 16 (over x, y).
Axes of the slice: x: 4, y: 4, z: 4, core: 2. Of those that a mesh axis runs over, the one named last changes fastest.
Arguments:
- left_edge: bfloat16 [16, 3072, 3072], P('row', 'col'), may hold values from -6 to 6
- right_edge: bfloat16 [16, 3072, 3072], P('row', 'col'), may hold values from -0.109375 to 0.109375
- projector: bfloat16 [16, 3072, 64], P('row'), may hold values from -0.109375 to 0.109375
- sector_size: int32 [16], P('row'), may hold values from 1 to 3072, 30720 in all
Outputs:
- enlarged: float32 [16, 3072, 3072], P('row', 'col')
- new_corner: float32 [16, 64, 64], P('row')
All inputs are finite; a program needn't handle non-finite values. No bound on the sum of `sector_size` on one device may be relied on, other than what follows from the above.
Results may differ from a plain program's by a relative error of at most 0.0003.
Values may be sent and summed in bfloat16 or wider, within the bound.
No kernel may reach another device: no remote copies, remote signals or barrier semaphores. Data moves between devices by JAX's collectives and lax.ppermute only.
A program may use at most 128 MiB of HBM per device.

v0:
```python
import jax
import jax.numpy as jnp
from jax import lax
from jax.sharding import PartitionSpec as P


def body(left_edge, right_edge, projector, sector_size):
    count = left_edge.shape[0]
    rows = left_edge.shape[1]
    width = projector.shape[1]
    kept = projector.shape[2]
    first_row = lax.axis_index("col") * rows
    states = jnp.arange(width, dtype=jnp.int32)
    live = (states[None, :] < sector_size[:, None]).astype(jnp.bfloat16)
    masked = projector * live[:, :, None]
    own_masked = lax.dynamic_slice_in_dim(masked, first_row, rows, 1).astype(jnp.float32)
    enlarged = jnp.einsum(
        "sik,skj->sij",
        left_edge,
        lax.all_gather(right_edge, "col", axis=1, tiled=True),
        preferred_element_type=jnp.float32,
    )
    inner = jnp.einsum(
        "sij,sjq->siq", enlarged, masked.astype(jnp.float32), precision=lax.Precision.HIGHEST
    )
    parts = jnp.einsum("sip,siq->spq", own_masked, inner, precision=lax.Precision.HIGHEST)
    entries = lax.axis_size("row") * count * kept * kept
    corner = lax.psum(parts, "col")
    total = lax.psum(jnp.sum(corner * corner), "row")
    return (enlarged, corner * lax.rsqrt(total / entries + 1e-06))


def solution(mesh):
    placed = (P("row", "col", None), P("row", "col", None), P("row", None, None), P("row"))
    return jax.shard_map(
        body,
        mesh=mesh,
        in_specs=placed,
        out_specs=(P("row", "col", None), P("row", None, None)),
        check_vma=False,
    )
```

profile of v0, /device:TPU:1, one launch (start us, length us, event | category | flops | bytes accessed | tf_op | source)
XLA Modules:
  0.0 348.4 jit_solution(8765672397625688852)
XLA Ops:
  7.2 0.0 copy-start
  7.2 0.0 all-gather.2.cloned.1.call-start
  7.2 0.7 all-gather.2.cloned.1.call-update
  7.9 0.7 compare_convert_fusion
  8.7 1.2 broadcast_multiply_fusion
  9.9 221.9 %all-gather.2.cloned.1.call-done = bf16[2,3072,3072]{2,1,0:T(8,128)(2,1)} async-done(((bf16[2,192,3072]{2,1,0:T(8,128)(2,1)}), bf16[2,3072,3072]{2,1,0:T(8,128)(2,1)}) %all-gather.2.cloned.1.call-update) | async-done | bytes 37748752 | tf_op jit(solution)/shard_map/all_gather | solution.py:20
  231.8 0.0 copy-done
  231.8 16.9 %fusion.3 = f32[2,192,3072]{2,1,0:T(8,128)} fusion(bf16[2,192,3072]{2,1,0:T(8,128)(2,1)S(1)} %copy-done, bf16[2,3072,3072]{2,1,0:T(8,128)(2,1)} %all-gather.2.cloned.1.call-done), kind=kOutput, calls=%fused_computation.7 | convolution fusion | flops 7247757312 | bytes 44826624 | tf_op jit(solution)/shard_map/sik,skj->sij/dot_general | solution.py:17
  248.6 5.0 %fusion.4 = f32[2,192,64]{1,2,0:T(8,128)S(1)} fusion(f32[2,192,3072]{2,1,0:T(8,128)} %fusion.3, bf16[2,3072,64]{1,2,0:T(8,128)(2,1)S(1)} %broadcast_multiply_fusion), kind=kOutput, calls=%fused_computation.8 | convolution fusion | flops 905969664 | bytes 5603328 | tf_op jit(solution)/shard_map/sij,sjq->siq/dot_general | solution.py:23
  253.6 0.3 fusion
  253.9 58.6 %psum.14 = f32[2,64,64]{2,1,0:T(8,128)S(1)} all-reduce(f32[2,64,64]{2,1,0:T(8,128)S(1)} %fusion), channel_id=1, replica_groups=mesh['row'=8,'col'=16] {'col'}, use_global_device_ids=true, to_apply=%region_0.0 | all-reduce | flops 8192 | bytes 65536 | tf_op jit(solution)/shard_map/psum | solution.py:28
  312.5 0.6 multiply_reduce_fusion
  313.1 27.0 %psum.15 = f32[]{:T(128)} all-reduce(f32[]{:T(128)} %multiply_reduce_fusion), channel_id=1, replica_groups=mesh['row'=8,'col'=16] {'row'}, use_global_device_ids=true, to_apply=%region_2.0 | all-reduce | flops 1 | bytes 8 | tf_op jit(solution)/shard_map/psum | solution.py:29
  340.9 0.6 broadcast_multiply_fusion.1
Async XLA Ops:
  7.2 224.6 %copy-start = (bf16[2,192,3072]{2,1,0:T(8,128)(2,1)S(1)}, bf16[2,192,3072]{2,1,0:T(8,128)(2,1)}, u32[]{:S(2)}) copy-start(bf16[2,192,3072]{2,1,0:T(8,128)(2,1)} %param.4) | copy-start | bytes 7077892
  7.2 224.6 %all-gather.2.cloned.1.call-start = ((), (), s32[]{:S(2)}) async-start(), calls=%async_computation | async-start | bytes 40108032 | tf_op jit(solution)/shard_map/all_gather | solution.py:20
Sparse Core Ops, SparseCore 0:
  10.2 221.5 all-gather.1
where the time goes:
time: 349 us; the launch traced here: 348 us
  waiting for transfers between devices  223 us (64%)
  blocking collectives  85.7 us (25%)
  matrix products  22.1 us (6%)
  between operations  14.7 us (4%)
    all_gather x1, waiting for transfers between devices, body(): lax.all_gather(right_edge, 'col', axis=1, tiled=True)  222 us
    psum x1, blocking collectives, body(): corner = lax.psum(parts, 'col')  58.6 us
    psum x1, blocking collectives, body(): total = lax.psum(jnp.sum(corner * corner), 'row')  27 us
    dot_general x1, matrix products, body(): jnp.einsum('sik,skj->sij', left_edge, lax.all_gather(right_edge, 'col', a...  16.9 us
  transfers between devices with their start and end apart: 1, of which 1 were waited for; matrix products, arithmetic and copies ran while one was open for 1% of the time, Pallas kernels for 0%

commit v1 on v0

--- a/solution.py
+++ b/solution.py
@@ -1,7 +1,15 @@
+import functools
 import jax
 import jax.numpy as jnp
 from jax import lax
 from jax.sharding import PartitionSpec as P
+
+
+def resolve_row(array_in, device_axis):
+    return jnp.sum(lax.all_gather(array_in, axis_name=device_axis), 0)
+
+
+ends_see = functools.partial(resolve_row, device_axis="col")
 
 
 def body(left_edge, right_edge, projector, sector_size):
@@ -25,7 +33,7 @@
     )
     parts = jnp.einsum("sip,siq->spq", own_masked, inner, precision=lax.Precision.HIGHEST)
     entries = lax.axis_size("row") * count * kept * kept
-    corner = lax.psum(parts, "col")
+    corner = ends_see(parts)
     total = lax.psum(jnp.sum(corner * corner), "row")
     return (enlarged, corner * lax.rsqrt(total / entries + 1e-06))
 

time: 349 us -> 300 us (0.86)
  blocking collectives: 85.7 us -> 37.5 us
    psum x1 -> x0, blocking collectives: 58.6 us -> none  [body(): corner = lax.psum(parts, 'col')]
    all_gather x0 -> x1, blocking collectives: none -> 19.3 us  [resolve_row(): return jnp.sum(lax.all_gather(array_in, axis_name=device_axis), 0)]
    psum x1, blocking collectives: 27 us -> 18.2 us  [body(): total = lax.psum(jnp.sum(corner * corner), 'row')]
where the time goes in v1:
time: 300 us
  waiting for transfers between devices  223 us (74%)
  blocking collectives  37.5 us (12%)
  matrix products  22.1 us (7%)
  between operations  14.7 us (5%)
  other arithmetic  3.27 us (1%)
    all_gather x1, waiting for transfers between devices, body(): lax.all_gather(right_edge, 'col', axis=1, tiled=True)  222 us
    all_gather x1, blocking collectives, resolve_row(): return jnp.sum(lax.all_gather(array_in, axis_name=device_axis), 0)  19.3 us
    psum x1, blocking collectives, body(): total = lax.psum(jnp.sum(corner * corner), 'row')  18.2 us
    dot_general x1, matrix products, body(): jnp.einsum('sik,skj->sij', left_edge, lax.all_gather(right_edge, 'col', a...  16.9 us
  transfers between devices with their start and end apart: 1, of which 1 were waited for; matrix products, arithmetic and copies ran while one was open for 1% of the time, Pallas kernels for 0%

profile of v1, /device:TPU:1, one launch (start us, length us, event | category | flops | bytes accessed | tf_op | source)
XLA Modules:
  0.0 300.2 jit_solution(6875226940043721463)
XLA Ops:
  7.2 0.0 copy-start
  7.2 0.0 all-gather.3.cloned.1.call-start
  7.2 0.7 all-gather.3.cloned.1.call-update
  7.9 0.7 compare_convert_fusion
  8.7 1.2 broadcast_multiply_fusion
  9.9 221.9 %all-gather.3.cloned.1.call-done = bf16[2,3072,3072]{2,1,0:T(8,128)(2,1)} async-done(((bf16[2,192,3072]{2,1,0:T(8,128)(2,1)}), bf16[2,3072,3072]{2,1,0:T(8,128)(2,1)}) %all-gather.3.cloned.1.call-update) | async-done | bytes 37748752 | tf_op jit(solution)/shard_map/all_gather | solution.py:28
  231.8 0.0 copy-done
  231.8 16.9 %fusion.3 = f32[2,192,3072]{2,1,0:T(8,128)} fusion(bf16[2,192,3072]{2,1,0:T(8,128)(2,1)S(1)} %copy-done, bf16[2,3072,3072]{2,1,0:T(8,128)(2,1)} %all-gather.3.cloned.1.call-done), kind=kOutput, calls=%fused_computation.7 | convolution fusion | flops 7247757312 | bytes 44826624 | tf_op jit(solution)/shard_map/sik,skj->sij/dot_general | solution.py:25
  248.6 5.0 %fusion.4 = f32[2,192,64]{1,2,0:T(8,128)S(1)} fusion(f32[2,192,3072]{2,1,0:T(8,128)} %fusion.3, bf16[2,3072,64]{1,2,0:T(8,128)(2,1)S(1)} %broadcast_multiply_fusion), kind=kOutput, calls=%fused_computation.8 | convolution fusion | flops 905969664 | bytes 5603328 | tf_op jit(solution)/shard_map/sij,sjq->siq/dot_general | solution.py:31
  253.6 0.3 fusion
  253.9 19.3 %all-gather = f32[32,64,64]{2,1,0:T(8,128)S(1)} all-gather(f32[2,64,64]{2,1,0:T(8,128)S(1)} %fusion), channel_id=2, replica_groups=mesh['row'=8,'col'=16] {'col'}, dimensions={0}, use_global_device_ids=true | all-gather | bytes 557056 | tf_op jit(solution)/shard_map/all_gather | solution.py:9
  273.2 0.1 reduce_sum.18
  273.3 0.6 multiply_reduce_fusion
  273.9 18.2 %psum.7 = f32[]{:T(128)} all-reduce(f32[]{:T(128)} %multiply_reduce_fusion), channel_id=1, replica_groups=mesh['row'=8,'col'=16] {'row'}, use_global_device_ids=true, to_apply=%region_2.0 | all-reduce | flops 1 | bytes 8 | tf_op jit(solution)/shard_map/psum | solution.py:37
  292.8 0.6 broadcast_multiply_fusion.1
Async XLA Ops:
  7.2 224.6 %copy-start = (bf16[2,192,3072]{2,1,0:T(8,128)(2,1)S(1)}, bf16[2,192,3072]{2,1,0:T(8,128)(2,1)}, u32[]{:S(2)}) copy-start(bf16[2,192,3072]{2,1,0:T(8,128)(2,1)} %param.4) | copy-start | bytes 7077892
  7.2 224.6 %all-gather.3.cloned.1.call-start = ((), (), s32[]{:S(2)}) async-start(), calls=%async_computation | async-start | bytes 40108032 | tf_op jit(solution)/shard_map/all_gather | solution.py:28
Sparse Core Ops, SparseCore 0:
  10.2 221.5 all-gather.2

commit v2 on v0

--- a/solution.py
+++ b/solution.py
@@ -1,7 +1,17 @@
+import functools
 import jax
 import jax.numpy as jnp
 from jax import lax
 from jax.sharding import PartitionSpec as P
+
+
+def supply_all_the_row(slab_in, bus_axis):
+    later = jnp.stack([slab_in for _ in range(jax.lax.axis_size(bus_axis))], axis=0)
+    known = jax.lax.all_to_all(later, axis_name=bus_axis, split_axis=0, concat_axis=0)
+    return jnp.concatenate(known, axis=1)
+
+
+assign_the_stages_all = functools.partial(supply_all_the_row, bus_axis="col")
 
 
 def body(left_edge, right_edge, projector, sector_size):
@@ -17,7 +27,7 @@
     enlarged = jnp.einsum(
         "sik,skj->sij",
         left_edge,
-        lax.all_gather(right_edge, "col", axis=1, tiled=True),
+        assign_the_stages_all(right_edge),
         preferred_element_type=jnp.float32,
     )
     inner = jnp.einsum(

time: 349 us -> 862 us (2.47)
  waiting for transfers between devices: 223 us -> 700 us
  local copies, waits for them, and re-layouts: 0.01 us -> 39.3 us
  between operations: 14.7 us -> 1.37 us
    all_to_all x0 -> x1, waiting for transfers between devices: none -> 700 us  [supply_all_the_row(): jax.lax.all_to_all(later, axis_name=bus_axis, split_axis=0, concat_axis=0)]
    all_gather x1 -> x0, waiting for transfers between devices: 222 us -> none  [body(): lax.all_gather(right_edge, 'col', axis=1, tiled=True)]
    reshape x0 -> x1, local copies, waits for them, and re-layouts: none -> 25.5 us  [supply_all_the_row(): return jnp.concatenate(known, axis=1)]
    another operation x0 -> x1, local copies, waits for them, and re-layouts: none -> 13.8 us  [supply_all_the_row(): jnp.stack([slab_in for _ in range(jax.lax.axis_size(bus_axis))], axis=0)]
  transfers between devices with their start and end apart: 1 -> 1, of which waited for: 1 -> 1; matrix products, arithmetic and copies ran while one was open for 1% -> 0% of each run, Pallas kernels for 0% -> 0%
where the time goes in v2:
time: 862 us
  waiting for transfers between devices  700 us (81%)
  blocking collectives  88.8 us (10%)
  local copies, waits for them, and re-layouts  39.3 us (5%)
  matrix products  22.1 us (3%)
    all_to_all x1, waiting for transfers between devices, supply_all_the_row(): jax.lax.all_to_all(later, axis_name=bus_axis, split_axis=0, concat_axis=0)  700 us
    psum x1, blocking collectives, body(): corner = lax.psum(parts, 'col')  59.5 us
    psum x1, blocking collectives, body(): total = lax.psum(jnp.sum(corner * corner), 'row')  29.3 us
    reshape x1, local copies, waits for them, and re-layouts, supply_all_the_row(): return jnp.concatenate(known, axis=1)  25.5 us
  transfers between devices with their start and end apart: 1, of which 1 were waited for; matrix products, arithmetic and copies ran while one was open for 0% of the time, Pallas kernels for 0%

profile of v2, /device:TPU:1, one launch (start us, length us, event | category | flops | bytes accessed | tf_op | source)
XLA Modules:
  0.0 861.8 jit_solution(1789313120721175357)
XLA Ops:
  0.6 0.0 copy-start
  0.6 13.8 %stack.2 = bf16[16,2,192,3072]{3,2,1,0:T(8,128)(2,1)} broadcast(bf16[2,192,3072]{2,1,0:T(8,128)(2,1)} %param.5), dimensions={1,2,3} | broadcast | bytes 40108032 | tf_op jit(solution)/shard_map/stack | solution.py:9
  14.4 0.0 copy-start.1
  14.4 7.8 all-to-all-start
  22.2 0.0 copy-done.1
  22.2 0.1 compare_convert_fusion
  22.3 1.2 broadcast_multiply_fusion
  23.5 699.9 %all-to-all-done = bf16[16,2,192,3072]{3,2,1,0:T(8,128)(2,1)} async-done(((bf16[16,2,192,3072]{3,2,1,0:T(8,128)(2,1)}), bf16[16,2,192,3072]{3,2,1,0:T(8,128)(2,1)}, u32[]{:S(2)}, u32[]{:S(2)}) %all-to-all-start) | async-done | bytes 37748768 | tf_op jit(solution)/shard_map/all_to_all | solution.py:10
  723.4 25.5 %copy.6 = bf16[2,16,192,3072]{3,2,1,0:T(8,128)(2,1)} copy(bf16[2,16,192,3072]{3,2,0,1:T(8,128)(2,1)} %bitcast) | data formatting | bytes 75497472 | tf_op jit(solution)/shard_map/reshape | solution.py:11
  748.9 0.0 copy-done
  748.9 16.9 %fusion.3 = f32[2,192,3072]{2,1,0:T(8,128)} fusion(bf16[2,192,3072]{2,1,0:T(8,128)(2,1)S(1)} %copy-done, bf16[2,3072,3072]{2,1,0:T(8,128)(2,1)} %bitcast.7), kind=kOutput, calls=%fused_computation.7 | convolution fusion | flops 7247757312 | bytes 44826624 | tf_op jit(solution)/shard_map/sik,skj->sij/dot_general | solution.py:27
  765.8 5.0 fusion.4
  770.8 0.3 fusion
  771.0 59.5 %psum.14 = f32[2,64,64]{2,1,0:T(8,128)S(1)} all-reduce(f32[2,64,64]{2,1,0:T(8,128)S(1)} %fusion), channel_id=1, replica_groups=mesh['row'=8,'col'=16] {'col'}, use_global_device_ids=true, to_apply=%region_0.0 | all-reduce | flops 8192 | bytes 65536 | tf_op jit(solution)/shard_map/psum | solution.py:38
  830.5 0.6 multiply_reduce_fusion
  831.2 29.3 %psum.15 = f32[]{:T(128)} all-reduce(f32[]{:T(128)} %multiply_reduce_fusion), channel_id=1, replica_groups=mesh['row'=8,'col'=16] {'row'}, use_global_device_ids=true, to_apply=%region_2.0 | all-reduce | flops 1 | bytes 8 | tf_op jit(solution)/shard_map/psum | solution.py:39
  861.2 0.6 broadcast_multiply_fusion.1
Async XLA Ops:
  0.6 748.2 %copy-start = (bf16[2,192,3072]{2,1,0:T(8,128)(2,1)S(1)}, bf16[2,192,3072]{2,1,0:T(8,128)(2,1)}, u32[]{:S(2)}) copy-start(bf16[2,192,3072]{2,1,0:T(8,128)(2,1)} %param.4) | copy-start | bytes 7077892
  14.4 7.8 copy-start.1
  14.4 709.0 %all-to-all-start = ((bf16[16,2,192,3072]{3,2,1,0:T(8,128)(2,1)}), bf16[16,2,192,3072]{3,2,1,0:T(8,128)(2,1)}, u32[]{:S(2)}, u32[]{:S(2)}) async-start(bf16[16,2,192,3072]{3,2,1,0:T(8,128)(2,1)} %stack.2), calls=%async_computation | async-start | bytes 75497472 | tf_op jit(solution)/shard_map/all_to_all | solution.py:10
